TPU v7x, 32 devices: a whole 2x2x4 slice. The times are simulated.
32 devices in a mesh: grp: 16 (over z, x, core), blk: 2 (over y).
Axes of the slice: x: 2, y: 2, z: 4, core: 2. Of those that a mesh axis runs over, the one named last changes fastest.
Arguments:
- walker_matrix: float32 [16, 2, 1024, 1024], P('grp', 'blk'), may hold values from -6 to 6
- updates: bfloat16 [16, 2, 4, 1024, 256], P('grp', 'blk'), may hold values from -0.19921875 to 0.19921875
- update_rows: int32 [16, 2, 4, 256], P('grp', 'blk'), may hold values from 0 to 1023, as said below
- left_table: float32 [1024, 256], replicated, may hold values from -0.1875 to 0.1875
- right_table: float32 [1024, 256], replicated, may hold values from -0.1875 to 0.1875
- assignment: int32 [2, 16], P('blk'), may hold values from 0 to 15, each once within a row
- momentum_sum: int32 [16, 16], replicated, may hold values from 0 to 15, as said below
- transfer_momentum: int32 [8], replicated, may hold values from 0 to 15
- transfer_frequency: int32 [8], replicated, may hold values from 0 to 15
- ownership: int32 [8], P('blk'), may hold values from 0 to 7, each once
- g4_prior: float32 [16, 8, 256, 256], P('grp', 'blk'), may hold values from -6 to 6
Outputs:
- g4_slices: float32 [16, 8, 256, 256], P('grp', 'blk')
Inputs may be any that keep to these rules, and one draw needn't show every extreme that they name: `update_rows`: within each update of each walker the 256 row indices are distinct. `assignment`: each row is a permutation of the grp indices. `momentum_sum`: the addition table of a periodic 4 x 4 cluster under a relabeling of its momenta; every row and column is a permutation. `ownership`: a permutation of the transfer slots.
All inputs are finite; a program needn't handle non-finite values.
Results may differ from a plain program's by a relative error of at most 0.0003.
Values sent between devices are 32-bit elements; how exact they have to be, the bound alone decides.
A program may use at most 128 MiB of HBM per device.

v0:
```python
import functools

import jax
import jax.numpy as jnp
from jax import lax
from jax.experimental import pallas as pl
from jax.experimental.pallas import tpu as pltpu
from jax.sharding import PartitionSpec as P

MESH = pl.DeviceIdType.MESH
F32 = jnp.float32
BF16 = jnp.bfloat16


def split(x):
    hi = x.astype(BF16)
    return hi, (x - hi.astype(F32)).astype(BF16)


def nn(a, b):
    return jnp.dot(a, b, preferred_element_type=F32)


def nt(a, b):
    return lax.dot_general(a, b, (((1,), (1,)), ((), ())), preferred_element_type=F32)


def partner_order(groups):
    return list(range(1, groups))


def exchange_kernel(
    groups, blocks, target_ref, own_ref, mom_ref, freq_ref, sum_ref, m_hbm, u_hbm, rows_hbm, l_hbm, r_hbm, prior_hbm, out_hbm,
    m_v, u_v, rows_v, l_v, r_v, pick_v, zh_v, zl_v, g_v, arranged, out_ref, perm_v, total_v, source,
    sems, out_sems, s1, r1, s2, r2, s3, r3, *spread,
):
    grp = lax.axis_index("grp")
    blk = lax.axis_index("blk")
    number, order, rank = u_v.shape
    halves, _, rows, kw = g_v.shape
    kh = kw // halves
    parts = 4
    step = order // parts

    pairs = partner_order(groups)

    def partner(i):
        place, bit = grp, 1
        while bit <= i:
            if i & bit:
                place = place + bit - 2 * bit * lax.rem(grp // bit, 2)
            bit *= 2
        return place

    def group_peer(i):
        return {"grp": partner(i), "blk": blk}

    def block_peer(i):
        return {"grp": grp, "blk": lax.rem(blk + i, blocks)}

    copy_rows = pltpu.make_async_copy(rows_hbm, rows_v, sems.at[0])
    copy_l = pltpu.make_async_copy(l_hbm, l_v, sems.at[1])
    copy_r = pltpu.make_async_copy(r_hbm, r_v, sems.at[2])
    copy_u = [pltpu.make_async_copy(u_hbm.at[i], u_v.at[i], sems.at[3 + i]) for i in range(number)]
    copy_m = [
        pltpu.make_async_copy(m_hbm.at[pl.ds(i * step, step)], m_v.at[pl.ds(i * step, step)], sems.at[3 + number + i])
        for i in range(parts)
    ]
    copy_rows.start()
    copy_l.start()
    for i in reversed(range(number)):
        copy_u[i].start()
    copy_r.start()
    for c in copy_m:
        c.start()
    copy_p = pltpu.make_async_copy(prior_hbm, total_v, sems.at[3 + number + parts])
    copy_p.start()

    barrier = pltpu.get_barrier_semaphore()

    for i in pairs:
        pl.semaphore_signal(barrier, inc=1, device_id=group_peer(i), device_id_type=MESH)

    @pl.loop(1, blocks)
    def _(i):
        pl.semaphore_signal(barrier, inc=1, device_id=block_peer(i), device_id_type=MESH)

    targets = [target_ref[0, w] for w in range(groups)]
    for a in range(groups):
        found = 0
        for w in range(groups):
            found = jnp.where(targets[w] == a, w, found)
        source[a] = found

    copy_rows.wait()
    for i in reversed(range(number)):
        pick_v[i] = jnp.where(
            lax.broadcasted_iota(jnp.int32, (order, rank), 0) == rows_v[pl.ds(i, 1), :], 1.0, 0.0
        ).astype(BF16)

    slots = total_v.shape[0]
    momenta = sum_ref.shape[0]
    nw = kw // momenta
    sub = lax.broadcasted_iota(jnp.int32, (nw, kw), 0)
    lane = lax.broadcasted_iota(jnp.int32, (nw, kw), 1)
    for j in range(slots):
        t = own_ref[j]
        q = mom_ref[t]
        moved = sub + freq_ref[t]
        base = lane - jnp.where(moved >= nw, moved - nw, moved)
        for kappa in range(momenta):
            hit = jnp.where(base == sum_ref[kappa, q] * nw, 1.0, 0.0).astype(BF16)
            perm_v[j * kw + kappa * nw:j * kw + (kappa + 1) * nw, :] = hit

    def accumulate(b, last):
        g = out_ref[b].reshape(kw, kw)
        gh, gl = split(g)
        xh = nt(perm_v[...], gh).astype(BF16)
        xl = nt(perm_v[...], gl).astype(BF16)
        for j in range(slots):
            rows_j = slice(j * kw, (j + 1) * kw)
            y = nt(jnp.concatenate([xh[rows_j], xl[rows_j]], axis=0), perm_v[rows_j, :])
            term = g * (y[:kw] + y[kw:])
            term = term * (1.0 / blocks)
            total_v[j] = total_v[j] + term
            if last:
                pltpu.make_async_copy(total_v.at[j], out_hbm.at[j], out_sems.at[j]).start()

    def chain(h):
        w = jnp.transpose(l_v[:, h * kh:(h + 1) * kh])
        for i in reversed(range(number)):
            if h == 0:
                copy_u[i].wait()
            t = nn(jnp.concatenate(split(w), axis=0), u_v[i])
            t = nt(jnp.concatenate(split(t[:kh] + t[kh:]), axis=0), pick_v[i])
            w = w + (t[:kh] + t[kh:])
        return split(w)

    def finish(h, wh, wl):
        t = nn(jnp.concatenate([wh, wl], axis=0), zh_v[...])
        g = t[:kh] + t[kh:] + nn(wh, zl_v[...])
        g_v[h] = g.reshape(groups, rows, kw)

    def first(h, i):
        return pltpu.make_async_remote_copy(
            g_v.at[h, partner(i)], spread[h].at[grp], s1.at[h, i], r1.at[h, i],
            device_id=group_peer(i), device_id_type=MESH)

    def second(h, i):
        return pltpu.make_async_remote_copy(
            arranged.at[h, partner(i)], out_ref.at[blk, h, grp], s2.at[h, i], r2.at[h, i],
            device_id=group_peer(i), device_id_type=MESH)

    def third(h, i, k):
        piece = out_ref.at[blk, h, partner(i)]
        return pltpu.make_async_remote_copy(
            piece, piece, s3.at[h, i, k], r3.at[h, i, k], device_id=block_peer(k), device_id_type=MESH)

    copy_l.wait()
    wh, wl = chain(0)
    copy_r.wait()
    rh, rl = split(r_v[...])
    for i in range(parts):
        copy_m[i].wait()
        mh, ml = split(m_v[pl.ds(i * step, step), :])
        t = nn(jnp.concatenate([mh, ml], axis=0), rh)
        zh, zl = split(t[:step] + t[step:] + nn(mh, rl))
        zh_v[pl.ds(i * step, step), :] = zh
        zl_v[pl.ds(i * step, step), :] = zl
    finish(0, wh, wl)

    pl.semaphore_wait(barrier, groups + blocks - 2)

    for h in range(halves):
        if h > 0:
            finish(h, *chain(h))

        for i in pairs:
            first(h, i).start()

        spread[h][grp] = g_v[h, grp]

    def forward(h, i):
        if i:
            second(h, i).wait_recv()
        for k in range(1, blocks):
            third(h, i, k).start()

    for h in range(halves):
        for i in pairs:
            first(h, i).wait_recv()
        out_ref[blk, h, grp] = spread[h][source[grp]]
        for i in pairs:
            a = partner(i)
            arranged[h, a] = spread[h][source[a]]
            second(h, i).start()
            if h > 0:
                forward(h - 1, i)
        forward(h, 0)
    for i in pairs:
        forward(halves - 1, i)

    copy_p.wait()
    accumulate(blk, blocks == 1)

    for k in range(1, blocks):
        for h in range(halves):
            for i in [0] + pairs:
                third(h, i, k).wait_recv()

        accumulate(lax.rem(blk + blocks - k, blocks), k == blocks - 1)

    for h in range(halves):
        for i in [0] + pairs:
            for k in range(1, blocks):
                third(h, i, k).wait_send()

        for i in pairs:
            first(h, i).wait_send()
            second(h, i).wait_send()

    for j in range(slots):
        pltpu.make_async_copy(total_v.at[j], out_hbm.at[j], out_sems.at[j]).wait()


def shards(
    walker_matrix,
    updates,
    update_rows,
    left_table,
    right_table,
    assignment,
    momentum_sum,
    transfer_momentum,
    transfer_frequency,
    ownership,
    g4_prior,
):
    groups = lax.axis_size("grp")
    blocks = lax.axis_size("blk")
    order, kw = left_table.shape
    number, rank = updates.shape[2], updates.shape[4]
    smem = pl.BlockSpec(memory_space=pltpu.SMEM)
    hbm = pl.BlockSpec(memory_space=pltpu.HBM)
    halves = 2 if kw // groups % 16 == 0 else 1
    rows = kw // groups // halves
    slots = g4_prior.shape[1]
    summed = pl.pallas_call(
        functools.partial(exchange_kernel, groups, blocks),
        out_shape=jax.ShapeDtypeStruct((slots, kw, kw), F32),
        in_specs=[smem] * 5 + [hbm] * 6,
        out_specs=hbm,
        scratch_shapes=[
            pltpu.VMEM((order, order), F32),
            pltpu.VMEM((number, order, rank), BF16),
            pltpu.VMEM((number, rank), jnp.int32),
            pltpu.VMEM((order, kw), F32),
            pltpu.VMEM((order, kw), F32),
            pltpu.VMEM((number, order, rank), BF16),
            pltpu.VMEM((order, kw), BF16),
            pltpu.VMEM((order, kw), BF16),
            pltpu.VMEM((halves, groups, rows, kw), F32),
            pltpu.VMEM((halves, groups, rows, kw), F32),
            pltpu.VMEM((blocks, halves, groups, rows, kw), F32),
            pltpu.VMEM((slots * kw, kw), BF16),
            pltpu.VMEM((slots, kw, kw), F32),
            pltpu.SMEM((groups,), jnp.int32),
            pltpu.SemaphoreType.DMA((number + 8,)),
            pltpu.SemaphoreType.DMA((slots,)),
            pltpu.SemaphoreType.DMA((halves, groups)),
            pltpu.SemaphoreType.DMA((halves, groups)),
            pltpu.SemaphoreType.DMA((halves, groups)),
            pltpu.SemaphoreType.DMA((halves, groups)),
            pltpu.SemaphoreType.DMA((halves, groups, blocks)),
            pltpu.SemaphoreType.DMA((halves, groups, blocks)),
        ] + [pltpu.VMEM((groups, rows, kw), F32)] * halves,
        compiler_params=pltpu.CompilerParams(
            collective_id=0, has_side_effects=True, vmem_limit_bytes=63 * 2**20 + 2**19),
        name="exchange",
    )(assignment, ownership, transfer_momentum, transfer_frequency, momentum_sum,
      walker_matrix[0, 0], updates[0, 0], update_rows[0, 0], left_table, right_table, g4_prior[0])
    return summed[None]


def solution(mesh):
    placed = (
        P("grp", "blk", None, None),
        P("grp", "blk", None, None, None),
        P("grp", "blk", None, None),
        P(),
        P(),
        P("blk", None),
        P(),
        P(),
        P(),
        P("blk"),
        P("grp", "blk", None, None),
    )
    return jax.shard_map(
        shards, mesh=mesh, in_specs=placed, out_specs=P("grp", "blk", None, None), check_vma=False
    )
```

profile of v0, /device:TPU:0, one launch (start us, length us, event | category | flops | bytes accessed | tf_op | source)
XLA Modules:
  0.0 36.5 jit_solution(7567287496762981216)
XLA Ops:
  0.0 34.2 %exchange.1 = f32[4,256,256]{2,1,0:T(8,128)} custom-call(s32[1,16]{1,0:T(1,128)} %target_ref.1, s32[4]{0:T(128)} %own_ref.1, s32[8]{0:T(128)} %mom_ref.1, s32[8]{0:T(128)} %freq_ref.1, s32[16,16]{1,0:T(8,128)} %sum_ref.1, f32[1024,1024]{1,0:T(8,128)} %bitcast.6, bf16[4,1024,256]{2,1,0:T(8,128)(2,1)} %bitcast.7, s32[4,256]{1,0:T(4,128)} %bitcast.9, ...), custom_call_target="tpu_custom_call" | custom-call | tf_op jit(solution)/shard_map/exchange/pallas_call | solution.py:248
  34.2 2.3 %copy.13 = f32[1,4,256,256]{3,2,1,0:T(8,128)} copy(f32[1,4,256,256]{3,2,1,0:T(8,128)} %bitcast.5) | data formatting | bytes 2097152
where the time goes:
time: 36.7 us; the launch traced here: 36.5 us
  Pallas kernels  34.2 us (93%)
  local copies, waits for them, and re-layouts  2.29 us (6%)
    pallas_call x1, Pallas kernels, shards(): pl.pallas_call(functools.partial(exchange_kernel, groups, blocks), out_sh...  34.2 us
    unnamed x1, local copies, waits for them, and re-layouts  2.29 us

commit v1 on v0

v1 whole, which is shorter than its diff:
```python
import functools

import jax
import jax.numpy as jnp
from jax import lax
from jax.experimental import pallas as pl
from jax.experimental.pallas import tpu as pltpu
from jax.sharding import PartitionSpec as P

MESH = pl.DeviceIdType.MESH
F32 = jnp.float32
BF16 = jnp.bfloat16


def split(x):
    hi = x.astype(BF16)
    return hi, (x - hi.astype(F32)).astype(BF16)


def nn(a, b):
    return jnp.dot(a, b, preferred_element_type=F32)


def nt(a, b):
    return lax.dot_general(a, b, (((1,), (1,)), ((), ())), preferred_element_type=F32)


def exchange_kernel(
    groups, blocks, target_ref, own_ref, mom_ref, freq_ref, sum_ref, m_hbm, u_hbm, rows_hbm, l_hbm, r_hbm, prior_hbm, out_ref,
    m_v, u_v, rows_v, l_v, r_v, pick_v, zh_v, zl_v, g_v, arranged, seen, perm_v, source,
    sems, s1, r1, s2, r2, s3, r3, *spread,
):
    grp = lax.axis_index("grp")
    blk = lax.axis_index("blk")
    number, order, rank = u_v.shape
    halves, cols, _, rows, width = g_v.shape
    kw = cols * width
    kh = kw // halves
    parts = 4
    step = order // parts
    slots = out_ref.shape[0]
    chunks = [(h, c) for h in range(halves) for c in range(cols)]
    pairs = list(range(1, groups))

    def partner(i):
        place, bit = grp, 1
        while bit <= i:
            if i & bit:
                place = place + bit - 2 * bit * lax.rem(grp // bit, 2)
            bit *= 2
        return place

    def group_peer(i):
        return {"grp": partner(i), "blk": blk}

    def block_peer(i):
        return {"grp": grp, "blk": lax.rem(blk + i, blocks)}

    copy_rows = pltpu.make_async_copy(rows_hbm, rows_v, sems.at[0])
    copy_l = pltpu.make_async_copy(l_hbm, l_v, sems.at[1])
    copy_r = pltpu.make_async_copy(r_hbm, r_v, sems.at[2])
    copy_p = pltpu.make_async_copy(prior_hbm, out_ref, sems.at[3])
    copy_u = [pltpu.make_async_copy(u_hbm.at[i], u_v.at[i], sems.at[4 + i]) for i in range(number)]
    copy_m = [
        pltpu.make_async_copy(m_hbm.at[pl.ds(i * step, step)], m_v.at[pl.ds(i * step, step)], sems.at[4 + number + i])
        for i in range(parts)
    ]
    copy_rows.start()
    copy_l.start()
    for i in reversed(range(number)):
        copy_u[i].start()
    copy_r.start()
    for c in copy_m:
        c.start()
    copy_p.start()

    barrier = pltpu.get_barrier_semaphore()

    for i in pairs:
        pl.semaphore_signal(barrier, inc=1, device_id=group_peer(i), device_id_type=MESH)

    @pl.loop(1, blocks)
    def _(i):
        pl.semaphore_signal(barrier, inc=1, device_id=block_peer(i), device_id_type=MESH)

    targets = [target_ref[0, w] for w in range(groups)]
    for a in range(groups):
        found = 0
        for w in range(groups):
            found = jnp.where(targets[w] == a, w, found)
        source[a] = found

    copy_rows.wait()
    for i in reversed(range(number)):
        pick_v[i] = jnp.where(
            lax.broadcasted_iota(jnp.int32, (order, rank), 0) == rows_v[pl.ds(i, 1), :], 1.0, 0.0
        ).astype(BF16)

    momenta = sum_ref.shape[0]
    nw = kw // momenta
    sub = lax.broadcasted_iota(jnp.int32, (nw, kw), 0)
    lane = lax.broadcasted_iota(jnp.int32, (nw, kw), 1)
    for j in range(slots):
        t = own_ref[j]
        q = mom_ref[t]
        moved = sub + freq_ref[t]
        base = lane - jnp.where(moved >= nw, moved - nw, moved)
        for kappa in range(momenta):
            hit = jnp.where(base == sum_ref[kappa, q] * nw, 1.0, 0.0).astype(BF16)
            perm_v[j * kw + kappa * nw:j * kw + (kappa + 1) * nw, :] = hit

    def accumulate(b):
        g = jnp.concatenate(
            [jnp.concatenate([seen[b, h, c].reshape(kh, width) for c in range(cols)], axis=1) for h in range(halves)],
            axis=0)
        gh, gl = split(g)
        xh = nt(perm_v[...], gh).astype(BF16)
        xl = nt(perm_v[...], gl).astype(BF16)
        for j in range(slots):
            rows_j = slice(j * kw, (j + 1) * kw)
            y = nt(jnp.concatenate([xh[rows_j], xl[rows_j]], axis=0), perm_v[rows_j, :])
            term = g * (y[:kw] + y[kw:])
            out_ref[j] = out_ref[j] + term * (1.0 / blocks)

    def chain(h):
        w = jnp.transpose(l_v[:, h * kh:(h + 1) * kh])
        for i in reversed(range(number)):
            if h == 0:
                copy_u[i].wait()
            t = nn(jnp.concatenate(split(w), axis=0), u_v[i])
            t = nt(jnp.concatenate(split(t[:kh] + t[kh:]), axis=0), pick_v[i])
            w = w + (t[:kh] + t[kh:])
        return split(w)

    def finish(h, wh, wl):
        t = nn(jnp.concatenate([wh, wl], axis=0), zh_v[...])
        g = t[:kh] + t[kh:] + nn(wh, zl_v[...])
        for c in range(cols):
            g_v[h, c] = g[:, c * width:(c + 1) * width].reshape(groups, rows, width)

    def first(k, i):
        h, c = chunks[k]
        return pltpu.make_async_remote_copy(
            g_v.at[h, c, partner(i)], spread[k].at[grp], s1.at[0], r1.at[k],
            device_id=group_peer(i), device_id_type=MESH)

    def second(k, i):
        h, c = chunks[k]
        return pltpu.make_async_remote_copy(
            arranged.at[h, c, partner(i)], seen.at[blk, h, c, grp], s2.at[0], r2.at[k],
            device_id=group_peer(i), device_id_type=MESH)

    def third(k, i):
        h, c = chunks[k]
        return pltpu.make_async_remote_copy(
            seen.at[blk, h, c], seen.at[blk, h, c], s3.at[0], r3.at[i],
            device_id=block_peer(i), device_id_type=MESH)

    def pieces(k, recv, send):
        h, c = chunks[k]
        return pltpu.make_async_remote_copy(
            arranged.at[h, c, pl.ds(0, groups - 1)], spread[k].at[pl.ds(0, groups - 1)], send, recv,
            device_id=block_peer(1), device_id_type=MESH)

    def whole(recv, send):
        return pltpu.make_async_remote_copy(
            seen.at[blk], seen.at[blk], send, recv, device_id=block_peer(1), device_id_type=MESH)

    copy_l.wait()
    wh, wl = chain(0)
    copy_r.wait()
    rh, rl = split(r_v[...])
    for i in range(parts):
        copy_m[i].wait()
        mh, ml = split(m_v[pl.ds(i * step, step), :])
        t = nn(jnp.concatenate([mh, ml], axis=0), rh)
        zh, zl = split(t[:step] + t[step:] + nn(mh, rl))
        zh_v[pl.ds(i * step, step), :] = zh
        zl_v[pl.ds(i * step, step), :] = zl
    finish(0, wh, wl)

    pl.semaphore_wait(barrier, groups + blocks - 2)

    for k, (h, c) in enumerate(chunks):
        if h > 0 and c == 0:
            finish(h, *chain(h))
        for i in pairs:
            first(k, i).start()
        spread[k][grp] = g_v[h, c, grp]

    for k, (h, c) in enumerate(chunks):
        pieces(k, r1.at[k], s1.at[0]).wait_recv()
        for i in pairs:
            a = partner(i)
            arranged[h, c, a] = spread[k][source[a]]
            second(k, i).start()
        seen[blk, h, c, grp] = spread[k][source[grp]]

    for k in range(len(chunks)):
        pieces(k, r2.at[k], s2.at[0]).wait_recv()
        for i in range(1, blocks):
            third(k, i).start()

    copy_p.wait()
    accumulate(blk)

    for i in range(1, blocks):
        whole(r3.at[i], s3.at[0]).wait_recv()
        accumulate(lax.rem(blk + blocks - i, blocks))

    for k in range(len(chunks)):
        pieces(k, r1.at[k], s1.at[0]).wait_send()
        pieces(k, r2.at[k], s2.at[0]).wait_send()
    for i in range(1, blocks):
        whole(r3.at[i], s3.at[0]).wait_send()


def shards(
    walker_matrix,
    updates,
    update_rows,
    left_table,
    right_table,
    assignment,
    momentum_sum,
    transfer_momentum,
    transfer_frequency,
    ownership,
    g4_prior,
):
    groups = lax.axis_size("grp")
    blocks = lax.axis_size("blk")
    order, kw = left_table.shape
    number, rank = updates.shape[2], updates.shape[4]
    smem = pl.BlockSpec(memory_space=pltpu.SMEM)
    hbm = pl.BlockSpec(memory_space=pltpu.HBM)
    halves = 2 if kw // groups % 16 == 0 else 1
    cols = 2 if kw % 256 == 0 else 1
    rows, width = kw // groups // halves, kw // cols
    slots = g4_prior.shape[1]
    room = 4 * slots * kw * kw
    summed = pl.pallas_call(
        functools.partial(exchange_kernel, groups, blocks),
        out_shape=pltpu.VMEM((slots, kw, kw), F32),
        in_specs=[smem] * 5 + [hbm] * 6,
        out_specs=pl.BlockSpec(memory_space=pltpu.VMEM),
        scratch_shapes=[
            pltpu.VMEM((order, order), F32),
            pltpu.VMEM((number, order, rank), BF16),
            pltpu.VMEM((number, rank), jnp.int32),
            pltpu.VMEM((order, kw), F32),
            pltpu.VMEM((order, kw), F32),
            pltpu.VMEM((number, order, rank), BF16),
            pltpu.VMEM((order, kw), BF16),
            pltpu.VMEM((order, kw), BF16),
            pltpu.VMEM((halves, cols, groups, rows, width), F32),
            pltpu.VMEM((halves, cols, groups, rows, width), F32),
            pltpu.VMEM((blocks, halves, cols, groups, rows, width), F32),
            pltpu.VMEM((slots * kw, kw), BF16),
            pltpu.SMEM((groups,), jnp.int32),
            pltpu.SemaphoreType.DMA((number + 8,)),
            pltpu.SemaphoreType.DMA((1,)),
            pltpu.SemaphoreType.DMA((halves * cols,)),
            pltpu.SemaphoreType.DMA((1,)),
            pltpu.SemaphoreType.DMA((halves * cols,)),
            pltpu.SemaphoreType.DMA((1,)),
            pltpu.SemaphoreType.DMA((blocks,)),
        ] + [pltpu.VMEM((groups, rows, width), F32)] * (halves * cols),
        compiler_params=pltpu.CompilerParams(
            collective_id=0, has_side_effects=True, vmem_limit_bytes=67043328 - room),
        name="exchange",
    )(assignment, ownership, transfer_momentum, transfer_frequency, momentum_sum,
      walker_matrix[0, 0], updates[0, 0], update_rows[0, 0], left_table, right_table, g4_prior[0])
    return summed[None]


def solution(mesh):
    placed = (
        P("grp", "blk", None, None),
        P("grp", "blk", None, None, None),
        P("grp", "blk", None, None),
        P(),
        P(),
        P("blk", None),
        P(),
        P(),
        P(),
        P("blk"),
        P("grp", "blk", None, None),
    )
    return jax.shard_map(
        shards, mesh=mesh, in_specs=placed, out_specs=P("grp", "blk", None, None), check_vma=False
    )
```

time: 36.7 us -> 34.7 us (0.946)
  local copies, waits for them, and re-layouts: 2.29 us -> 0.97 us
  Pallas kernels: 34.2 us -> 33.5 us
    unnamed x1, local copies, waits for them, and re-layouts: 2.29 us -> 0.97 us
    pallas_call x1, Pallas kernels: 34.2 us -> 33.5 us  [shards(): pl.pallas_call(functools.partial(exchange_kernel, groups, blocks), out_sh...]
where the time goes in v1:
time: 34.7 us; the launch traced here: 34.5 us
  Pallas kernels  33.5 us (97%)
  local copies, waits for them, and re-layouts  0.97 us (3%)
    pallas_call x1, Pallas kernels, shards(): pl.pallas_call(functools.partial(exchange_kernel, groups, blocks), out_sh...  33.5 us
    unnamed x1, local copies, waits for them, and re-layouts  0.97 us

profile of v1, /device:TPU:0, one launch (start us, length us, event | category | flops | bytes accessed | tf_op | source)
XLA Modules:
  0.0 34.5 jit_solution(8584692858355494303)
XLA Ops:
  0.0 33.5 %exchange.1 = f32[4,256,256]{2,1,0:T(8,128)S(1)} custom-call(s32[1,16]{1,0:T(1,128)} %target_ref.1, s32[4]{0:T(128)} %own_ref.1, s32[8]{0:T(128)} %mom_ref.1, s32[8]{0:T(128)} %freq_ref.1, s32[16,16]{1,0:T(8,128)} %sum_ref.1, f32[1024,1024]{1,0:T(8,128)} %bitcast.6, bf16[4,1024,256]{2,1,0:T(8,128)(2,1)} %bitcast.7, s32[4,256]{1,0:T(4,128)} %bitcast.9, ...), custom_call_target="tpu_custom_call" | custom-call | tf_op jit(solution)/shard_map/exchange/pallas_call | solution.py:242
  33.5 1.0 %copy.13 = f32[1,4,256,256]{3,2,1,0:T(8,128)} copy(f32[1,4,256,256]{3,2,1,0:T(8,128)S(1)} %bitcast.5) | data formatting | bytes 2097152

commit v2 on v1

v2 whole, which is shorter than its diff:
```python
import functools

import jax
import jax.numpy as jnp
from jax import lax
from jax.experimental import pallas as pl
from jax.experimental.pallas import tpu as pltpu
from jax.sharding import PartitionSpec as P

MESH = pl.DeviceIdType.MESH
F32 = jnp.float32
BF16 = jnp.bfloat16


def split(x):
    hi = x.astype(BF16)
    return hi, (x - hi.astype(F32)).astype(BF16)


def nn(a, b):
    return jnp.dot(a, b, preferred_element_type=F32)


def nt(a, b):
    return lax.dot_general(a, b, (((1,), (1,)), ((), ())), preferred_element_type=F32)


def exchange_kernel(
    groups, blocks, target_hbm, own_hbm, mom_hbm, freq_hbm, sum_hbm, m_hbm, u_hbm, rows_hbm, l_hbm, r_hbm, prior_hbm, out_ref,
    target_ref, own_ref, mom_ref, freq_ref, sum_ref, m_v, u_v, rows_v, l_v, r_v, pick_v, rh_v, rl_v, zh_v, zl_v, g_v, arranged, seen, perm_v, part_v, source,
    sems, s1, r1, s2, r2, s3, r3, s4, r4, *spread,
):
    grp = lax.axis_index("grp")
    blk = lax.axis_index("blk")
    number, order, rank = u_v.shape
    halves, cols, _, rows, width = g_v.shape
    kw = cols * width
    kh = kw // halves
    parts = 4
    step = order // parts
    slots = out_ref.shape[0]
    chunks = [(h, c) for h in range(halves) for c in range(cols)]
    pairs = list(range(1, groups))

    def partner(i):
        place, bit = grp, 1
        while bit <= i:
            if i & bit:
                place = place + bit - 2 * bit * lax.rem(grp // bit, 2)
            bit *= 2
        return place

    def group_peer(i):
        return {"grp": partner(i), "blk": blk}

    def block_peer(i):
        return {"grp": grp, "blk": lax.rem(blk + i, blocks)}

    copy_rows = pltpu.make_async_copy(rows_hbm, rows_v, sems.at[0])
    copy_l = pltpu.make_async_copy(l_hbm, l_v, sems.at[1])
    copy_r = pltpu.make_async_copy(r_hbm, r_v, sems.at[2])
    copy_p = pltpu.make_async_copy(prior_hbm, out_ref, sems.at[3])
    copy_u = [pltpu.make_async_copy(u_hbm.at[i], u_v.at[i], sems.at[4 + i]) for i in range(number)]
    copy_m = [
        pltpu.make_async_copy(m_hbm.at[pl.ds(i * step, step)], m_v.at[pl.ds(i * step, step)], sems.at[4 + number + i])
        for i in range(parts)
    ]
    copy_rows.start()
    copy_l.start()
    copy_u[number - 1].start()
    copy_r.start()
    copy_m[0].start()

    small = [(target_hbm, target_ref), (own_hbm, own_ref), (mom_hbm, mom_ref), (freq_hbm, freq_ref), (sum_hbm, sum_ref)]
    small = [pltpu.make_async_copy(a, b, sems.at[4 + number + parts + i]) for i, (a, b) in enumerate(small)]
    for c in small:
        c.start()

    barrier = pltpu.get_barrier_semaphore()

    for i in pairs:
        pl.semaphore_signal(barrier, inc=1, device_id=group_peer(i), device_id_type=MESH)

    @pl.loop(1, blocks)
    def _(i):
        pl.semaphore_signal(barrier, inc=1, device_id=block_peer(i), device_id_type=MESH)

    copy_rows.wait()
    for i in reversed(range(number)):
        pick_v[i] = jnp.where(
            lax.broadcasted_iota(jnp.int32, (order, rank), 0) == rows_v[pl.ds(i, 1), :], 1.0, 0.0
        ).astype(BF16)

    def rows_of(b, h):
        return jnp.concatenate([seen[b, h, c].reshape(kh, width) for c in range(cols)], axis=1)

    def accumulate(b, h):
        x = nt(perm_v[...], jnp.concatenate(split(rows_of(b, h)), axis=0)).astype(BF16)
        last = h == halves - 1
        if last:
            g = jnp.concatenate([rows_of(b, i) for i in range(halves)], axis=0)
        for j in range(slots):
            here = slice(j * kw, (j + 1) * kw)
            p = perm_v[here, h * kh:(h + 1) * kh]
            y = nt(x[here], jnp.concatenate([p, p], axis=1))
            if h > 0:
                y = y + part_v[b, j]
            if last:
                out_ref[j] = out_ref[j] + g * y * (1.0 / blocks)
            else:
                part_v[b, j] = y

    def apply(h, w, i, between=None):
        t = nn(jnp.concatenate(split(w), axis=0), u_v[i])
        if between:
            between()
        t = nt(jnp.concatenate(split(t[:kh] + t[kh:]), axis=0), pick_v[i])
        return w + (t[:kh] + t[kh:])

    def project(i):
        mh, ml = split(m_v[pl.ds(i * step, step), :])
        t = nn(jnp.concatenate([mh, ml], axis=0), rh_v[...])
        zh, zl = split(t[:step] + t[step:] + nn(mh, rl_v[...]))
        zh_v[pl.ds(i * step, step), :] = zh
        zl_v[pl.ds(i * step, step), :] = zl

    def finish(h, wh, wl):
        t = nn(jnp.concatenate([wh, wl], axis=0), zh_v[...])
        g = t[:kh] + t[kh:] + nn(wh, zl_v[...])
        for c in range(cols):
            g_v[h, c] = g[:, c * width:(c + 1) * width].reshape(groups, rows, width)

    def first(k, i):
        h, c = chunks[k]
        return pltpu.make_async_remote_copy(
            g_v.at[h, c, partner(i)], spread[k].at[grp], s1.at[0], r1.at[k],
            device_id=group_peer(i), device_id_type=MESH)

    def second(k, i):
        h, c = chunks[k]
        return pltpu.make_async_remote_copy(
            arranged.at[h, c, partner(i)], seen.at[blk, h, c, grp], s2.at[0], r2.at[k],
            device_id=group_peer(i), device_id_type=MESH)

    def third(k, i):
        h, c = chunks[k]
        return pltpu.make_async_remote_copy(
            seen.at[blk, h, c], seen.at[blk, h, c], s3.at[0], r3.at[i],
            device_id=block_peer(i), device_id_type=MESH)

    def across(c, i, j):
        return pltpu.make_async_remote_copy(
            arranged.at[halves - 1, c, partner(i)], seen.at[blk, halves - 1, c, grp], s4.at[0], r4.at[j, c],
            device_id={"grp": partner(i), "blk": lax.rem(blk + j, blocks)}, device_id_type=MESH)

    def pieces(k, recv, send):
        h, c = chunks[k]
        return pltpu.make_async_remote_copy(
            arranged.at[h, c, pl.ds(0, groups - 1)], spread[k].at[pl.ds(0, groups - 1)], send, recv,
            device_id=block_peer(1), device_id_type=MESH)

    def quarter(c, recv, send):
        return pltpu.make_async_remote_copy(
            arranged.at[halves - 1, c], seen.at[blk, halves - 1, c], send, recv, device_id=block_peer(1), device_id_type=MESH)

    def early(recv, send):
        return pltpu.make_async_remote_copy(
            seen.at[blk, pl.ds(0, halves - 1)], seen.at[blk, pl.ds(0, halves - 1)], send, recv,
            device_id=block_peer(1), device_id_type=MESH)

    copy_l.wait()
    copy_u[number - 1].wait()
    later = [copy_u[number - 2], copy_m[1], copy_u[number - 3], copy_m[2], copy_u[number - 4], copy_m[3], copy_p]
    for c in later[:4]:
        c.start()
    w = apply(0, jnp.transpose(l_v[:, :kh]), number - 1)
    copy_r.wait()
    rh_v[...], rl_v[...] = split(r_v[...])
    for i in range(parts):
        for c in later[4 + 2 * i:4 + 2 * i + 2]:
            c.start()
        copy_m[i].wait()
        u = number - 2 - i
        if u >= 0:
            copy_u[u].wait()
            w = apply(0, w, u, functools.partial(project, i))
        else:
            project(i)
    finish(0, *split(w))

    pl.semaphore_wait(barrier, groups + blocks - 2)

    for k, (h, c) in enumerate(chunks):
        if h > 0 and c == 0:
            w = jnp.transpose(l_v[:, h * kh:(h + 1) * kh])
            for i in reversed(range(number)):
                w = apply(h, w, i)
            finish(h, *split(w))
        for i in pairs:
            first(k, i).start()
        spread[k][grp] = g_v[h, c, grp]

    for c in small:
        c.wait()
    targets = [target_ref[0, w] for w in range(groups)]
    for a in range(groups):
        found = 0
        for w in range(groups):
            found = jnp.where(targets[w] == a, w, found)
        source[a] = found

    momenta = sum_ref.shape[0]
    nw = kw // momenta
    sub = lax.broadcasted_iota(jnp.int32, (nw, kw), 0)
    lane = lax.broadcasted_iota(jnp.int32, (nw, kw), 1)
    for j in range(slots):
        t = own_ref[j]
        q = mom_ref[t]
        moved = sub + freq_ref[t]
        base = lane - jnp.where(moved >= nw, moved - nw, moved)
        for kappa in range(momenta):
            hit = jnp.where(base == sum_ref[kappa, q] * nw, 1.0, 0.0).astype(BF16)
            perm_v[j * kw + kappa * nw:j * kw + (kappa + 1) * nw, :] = hit

    for k, (h, c) in enumerate(chunks):
        pieces(k, r1.at[k], s1.at[0]).wait_recv()
        for i in pairs:
            a = partner(i)
            arranged[h, c, a] = spread[k][source[a]]
            if h == halves - 1:
                for j in range(1, blocks):
                    across(c, i, j).start()
            second(k, i).start()
        mine = spread[k][source[grp]]
        seen[blk, h, c, grp] = mine
        if h == halves - 1:
            arranged[h, c, grp] = mine
            for j in range(1, blocks):
                across(c, 0, j).start()

    for k, (h, c) in enumerate(chunks):
        if h < halves - 1:
            pieces(k, r2.at[k], s2.at[0]).wait_recv()
            for j in range(1, blocks):
                third(k, j).start()

    def other(j):
        return lax.rem(blk + blocks - j, blocks)

    if halves > 1:
        for h in range(halves - 1):
            accumulate(blk, h)
        for j in range(1, blocks):
            early(r3.at[j], s3.at[0]).wait_recv()
            for h in range(halves - 1):
                accumulate(other(j), h)

    copy_p.wait()
    for k, (h, c) in enumerate(chunks):
        if h == halves - 1:
            pieces(k, r2.at[k], s2.at[0]).wait_recv()
    accumulate(blk, halves - 1)
    for j in range(1, blocks):
        for c in range(cols):
            quarter(c, r4.at[j, c], s4.at[0]).wait_recv()
        accumulate(other(j), halves - 1)

    for k in range(len(chunks)):
        pieces(k, r1.at[k], s1.at[0]).wait_send()
        pieces(k, r2.at[k], s2.at[0]).wait_send()
    for j in range(1, blocks):
        if halves > 1:
            early(r3.at[j], s3.at[0]).wait_send()
        for c in range(cols):
            quarter(c, r4.at[j, c], s4.at[0]).wait_send()


def shards(
    walker_matrix,
    updates,
    update_rows,
    left_table,
    right_table,
    assignment,
    momentum_sum,
    transfer_momentum,
    transfer_frequency,
    ownership,
    g4_prior,
):
    groups = lax.axis_size("grp")
    blocks = lax.axis_size("blk")
    order, kw = left_table.shape
    number, rank = updates.shape[2], updates.shape[4]
    hbm = pl.BlockSpec(memory_space=pltpu.HBM)
    halves = 2 if kw // groups % 16 == 0 else 1
    cols = 2 if kw % 256 == 0 else 1
    rows, width = kw // groups // halves, kw // cols
    slots = g4_prior.shape[1]
    room = 4 * slots * kw * kw
    summed = pl.pallas_call(
        functools.partial(exchange_kernel, groups, blocks),
        out_shape=pltpu.VMEM((slots, kw, kw), F32),
        in_specs=[hbm] * 11,
        out_specs=pl.BlockSpec(memory_space=pltpu.VMEM),
        scratch_shapes=[
            pltpu.SMEM(assignment.shape, jnp.int32),
            pltpu.SMEM(ownership.shape, jnp.int32),
            pltpu.SMEM(transfer_momentum.shape, jnp.int32),
            pltpu.SMEM(transfer_frequency.shape, jnp.int32),
            pltpu.SMEM(momentum_sum.shape, jnp.int32),
            pltpu.VMEM((order, order), F32),
            pltpu.VMEM((number, order, rank), BF16),
            pltpu.VMEM((number, rank), jnp.int32),
            pltpu.VMEM((order, kw), F32),
            pltpu.VMEM((order, kw), F32),
            pltpu.VMEM((number, order, rank), BF16),
            pltpu.VMEM((order, kw), BF16),
            pltpu.VMEM((order, kw), BF16),
            pltpu.VMEM((order, kw), BF16),
            pltpu.VMEM((order, kw), BF16),
            pltpu.VMEM((halves, cols, groups, rows, width), F32),
            pltpu.VMEM((halves, cols, groups, rows, width), F32),
            pltpu.VMEM((blocks, halves, cols, groups, rows, width), F32),
            pltpu.VMEM((slots * kw, kw), BF16),
            pltpu.VMEM((blocks, slots, kw, kw), F32),
            pltpu.SMEM((groups,), jnp.int32),
            pltpu.SemaphoreType.DMA((number + 13,)),
            pltpu.SemaphoreType.DMA((1,)),
            pltpu.SemaphoreType.DMA((halves * cols,)),
            pltpu.SemaphoreType.DMA((1,)),
            pltpu.SemaphoreType.DMA((halves * cols,)),
            pltpu.SemaphoreType.DMA((1,)),
            pltpu.SemaphoreType.DMA((blocks,)),
            pltpu.SemaphoreType.DMA((1,)),
            pltpu.SemaphoreType.DMA((blocks, cols)),
        ] + [pltpu.VMEM((groups, rows, width), F32)] * (halves * cols),
        compiler_params=pltpu.CompilerParams(
            collective_id=0, has_side_effects=True, vmem_limit_bytes=67043328 - room),
        name="exchange",
    )(assignment, ownership, transfer_momentum, transfer_frequency, momentum_sum,
      walker_matrix[0, 0], updates[0, 0], update_rows[0, 0], left_table, right_table, g4_prior[0])
    return summed[None]


def solution(mesh):
    placed = (
        P("grp", "blk", None, None),
        P("grp", "blk", None, None, None),
        P("grp", "blk", None, None),
        P(),
        P(),
        P("blk", None),
        P(),
        P(),
        P(),
        P("blk"),
        P("grp", "blk", None, None),
    )
    return jax.shard_map(
        shards, mesh=mesh, in_specs=placed, out_specs=P("grp", "blk", None, None), check_vma=False
    )
```

time: 34.7 us -> 30.7 us (0.88)
  Pallas kernels: 33.5 us -> 29.5 us
    pallas_call x1, Pallas kernels: 33.5 us -> 29.5 us  [shards(): pl.pallas_call(functools.partial(exchange_kernel, groups, blocks), out_sh...]
where the time goes in v2:
time: 30.7 us; the launch traced here: 30.5 us
  Pallas kernels  29.5 us (96%)
  local copies, waits for them, and re-layouts  0.97 us (3%)
    pallas_call x1, Pallas kernels, shards(): pl.pallas_call(functools.partial(exchange_kernel, groups, blocks), out_sh...  29.5 us
    unnamed x1, local copies, waits for them, and re-layouts  0.97 us

profile of v2, /device:TPU:0, one launch (start us, length us, event | category | flops | bytes accessed | tf_op | source)
XLA Modules:
  0.0 30.5 jit_solution(8865666707679363326)
XLA Ops:
  0.0 29.5 %exchange.1 = f32[4,256,256]{2,1,0:T(8,128)S(1)} custom-call(s32[1,16]{1,0:T(1,128)} %target_hbm.1, s32[4]{0:T(128)} %own_hbm.1, s32[8]{0:T(128)} %mom_hbm.1, s32[8]{0:T(128)} %freq_hbm.1, s32[16,16]{1,0:T(8,128)} %sum_hbm.1, f32[1024,1024]{1,0:T(8,128)} %bitcast.6, bf16[4,1024,256]{2,1,0:T(8,128)(2,1)} %bitcast.7, s32[4,256]{1,0:T(4,128)} %bitcast.9, ...), custom_call_target="tpu_custom_call" | custom-call | tf_op jit(solution)/shard_map/exchange/pallas_call | solution.py:301
  29.5 1.0 %copy.13 = f32[1,4,256,256]{3,2,1,0:T(8,128)} copy(f32[1,4,256,256]{3,2,1,0:T(8,128)S(1)} %bitcast.5) | data formatting | bytes 2097152

commit v3 on v2

--- a/solution.py
+++ b/solution.py
@@ -28,7 +28,7 @@
 def exchange_kernel(
     groups, blocks, target_hbm, own_hbm, mom_hbm, freq_hbm, sum_hbm, m_hbm, u_hbm, rows_hbm, l_hbm, r_hbm, prior_hbm, out_ref,
     target_ref, own_ref, mom_ref, freq_ref, sum_ref, m_v, u_v, rows_v, l_v, r_v, pick_v, rh_v, rl_v, zh_v, zl_v, g_v, arranged, seen, perm_v, part_v, source,
-    sems, s1, r1, s2, r2, s3, r3, s4, r4, *spread,
+    sems, s1, r1, s2, r2, s3, r3, *spread,
 ):
     grp = lax.axis_index("grp")
     blk = lax.axis_index("blk")
@@ -70,6 +70,9 @@
     copy_u[number - 1].start()
     copy_r.start()
     copy_m[0].start()
+    later = [copy_u[number - 2], copy_m[1], copy_u[number - 3], copy_m[2], copy_u[number - 4], copy_m[3], copy_p]
+    for c in later:
+        c.start()
 
     small = [(target_hbm, target_ref), (own_hbm, own_ref), (mom_hbm, mom_ref), (freq_hbm, freq_ref), (sum_hbm, sum_ref)]
     small = [pltpu.make_async_copy(a, b, sems.at[4 + number + parts + i]) for i, (a, b) in enumerate(small)]
@@ -142,15 +145,16 @@
             arranged.at[h, c, partner(i)], seen.at[blk, h, c, grp], s2.at[0], r2.at[k],
             device_id=group_peer(i), device_id_type=MESH)
 
-    def third(k, i):
-        h, c = chunks[k]
-        return pltpu.make_async_remote_copy(
-            seen.at[blk, h, c], seen.at[blk, h, c], s3.at[0], r3.at[i],
-            device_id=block_peer(i), device_id_type=MESH)
-
-    def across(c, i, j):
-        return pltpu.make_async_remote_copy(
-            arranged.at[halves - 1, c, partner(i)], seen.at[blk, halves - 1, c, grp], s4.at[0], r4.at[j, c],
+    def third(k, j):
+        h, c = chunks[k]
+        return pltpu.make_async_remote_copy(
+            seen.at[blk, h, c], seen.at[blk, h, c], s3.at[0], r3.at[j, k],
+            device_id=block_peer(j), device_id_type=MESH)
+
+    def across(k, i, j):
+        h, c = chunks[k]
+        return pltpu.make_async_remote_copy(
+            arranged.at[h, c, partner(i)], seen.at[blk, h, c, grp], s3.at[0], r3.at[j, k],
             device_id={"grp": partner(i), "blk": lax.rem(blk + j, blocks)}, device_id_type=MESH)
 
     def pieces(k, recv, send):
@@ -159,33 +163,23 @@
             arranged.at[h, c, pl.ds(0, groups - 1)], spread[k].at[pl.ds(0, groups - 1)], send, recv,
             device_id=block_peer(1), device_id_type=MESH)
 
-    def quarter(c, recv, send):
-        return pltpu.make_async_remote_copy(
-            arranged.at[halves - 1, c], seen.at[blk, halves - 1, c], send, recv, device_id=block_peer(1), device_id_type=MESH)
-
-    def early(recv, send):
-        return pltpu.make_async_remote_copy(
-            seen.at[blk, pl.ds(0, halves - 1)], seen.at[blk, pl.ds(0, halves - 1)], send, recv,
-            device_id=block_peer(1), device_id_type=MESH)
+    direct = (2, 3)
 
     copy_l.wait()
     copy_u[number - 1].wait()
-    later = [copy_u[number - 2], copy_m[1], copy_u[number - 3], copy_m[2], copy_u[number - 4], copy_m[3], copy_p]
-    for c in later[:4]:
-        c.start()
+    copy_r.wait()
+    copy_m[0].wait()
     w = apply(0, jnp.transpose(l_v[:, :kh]), number - 1)
-    copy_r.wait()
     rh_v[...], rl_v[...] = split(r_v[...])
     for i in range(parts):
-        for c in later[4 + 2 * i:4 + 2 * i + 2]:
-            c.start()
-        copy_m[i].wait()
-        u = number - 2 - i
-        if u >= 0:
-            copy_u[u].wait()
+        if i == 1:
+            for c in copy_m[1:] + copy_u[:number - 1]:
+                c.wait()
+        u = number - 1 - i
+        if i == 0:
+            project(0)
+        else:
             w = apply(0, w, u, functools.partial(project, i))
-        else:
-            project(i)
     finish(0, *split(w))
 
     pl.semaphore_wait(barrier, groups + blocks - 2)
@@ -227,52 +221,43 @@
         for i in pairs:
             a = partner(i)
             arranged[h, c, a] = spread[k][source[a]]
-            if h == halves - 1:
+            second(k, i).start()
+            if k in direct:
                 for j in range(1, blocks):
-                    across(c, i, j).start()
-            second(k, i).start()
+                    across(k, i, j).start()
         mine = spread[k][source[grp]]
         seen[blk, h, c, grp] = mine
-        if h == halves - 1:
+        if k in direct:
             arranged[h, c, grp] = mine
             for j in range(1, blocks):
-                across(c, 0, j).start()
-
-    for k, (h, c) in enumerate(chunks):
-        if h < halves - 1:
+                across(k, 0, j).start()
+
+    def other(j):
+        return lax.rem(blk + blocks - j, blocks)
+
+    for k in range(len(chunks)):
+        if k not in direct:
             pieces(k, r2.at[k], s2.at[0]).wait_recv()
             for j in range(1, blocks):
                 third(k, j).start()
 
-    def other(j):
-        return lax.rem(blk + blocks - j, blocks)
-
-    if halves > 1:
-        for h in range(halves - 1):
-            accumulate(blk, h)
+    copy_p.wait()
+    for h in range(halves):
+        now = [k for k in range(len(chunks)) if chunks[k][0] == h]
+        for k in now:
+            if k in direct:
+                pieces(k, r2.at[k], s2.at[0]).wait_recv()
+        accumulate(blk, h)
         for j in range(1, blocks):
-            early(r3.at[j], s3.at[0]).wait_recv()
-            for h in range(halves - 1):
-                accumulate(other(j), h)
-
-    copy_p.wait()
-    for k, (h, c) in enumerate(chunks):
-        if h == halves - 1:
-            pieces(k, r2.at[k], s2.at[0]).wait_recv()
-    accumulate(blk, halves - 1)
-    for j in range(1, blocks):
-        for c in range(cols):
-            quarter(c, r4.at[j, c], s4.at[0]).wait_recv()
-        accumulate(other(j), halves - 1)
+            for k in now:
+                third(k, j).wait_recv()
+            accumulate(other(j), h)
 
     for k in range(len(chunks)):
         pieces(k, r1.at[k], s1.at[0]).wait_send()
         pieces(k, r2.at[k], s2.at[0]).wait_send()
-    for j in range(1, blocks):
-        if halves > 1:
-            early(r3.at[j], s3.at[0]).wait_send()
-        for c in range(cols):
-            quarter(c, r4.at[j, c], s4.at[0]).wait_send()
+        for j in range(1, blocks):
+            third(k, j).wait_send()
 
 
 def shards(
@@ -331,9 +316,7 @@
             pltpu.SemaphoreType.DMA((1,)),
             pltpu.SemaphoreType.DMA((halves * cols,)),
             pltpu.SemaphoreType.DMA((1,)),
-            pltpu.SemaphoreType.DMA((blocks,)),
-            pltpu.SemaphoreType.DMA((1,)),
-            pltpu.SemaphoreType.DMA((blocks, cols)),
+            pltpu.SemaphoreType.DMA((blocks, halves * cols)),
         ] + [pltpu.VMEM((groups, rows, width), F32)] * (halves * cols),
         compiler_params=pltpu.CompilerParams(
             collective_id=0, has_side_effects=True, vmem_limit_bytes=67043328 - room),

time: 30.7 us -> 29.7 us (0.967)
  Pallas kernels: 29.5 us -> 28.6 us
    pallas_call x1, Pallas kernels: 29.5 us -> 28.6 us  [shards(): pl.pallas_call(functools.partial(exchange_kernel, groups, blocks), out_sh...]
where the time goes in v3:
time: 29.7 us; the launch traced here: 29.5 us
  Pallas kernels  28.6 us (96%)
  local copies, waits for them, and re-layouts  0.97 us (3%)
    pallas_call x1, Pallas kernels, shards(): pl.pallas_call(functools.partial(exchange_kernel, groups, blocks), out_sh...  28.6 us
    unnamed x1, local copies, waits for them, and re-layouts  0.97 us

profile of v3, /device:TPU:0, one launch (start us, length us, event | category | flops | bytes accessed | tf_op | source)
XLA Modules:
  0.0 29.5 jit_solution(2078564873436059675)
XLA Ops:
  0.0 28.6 %exchange.1 = f32[4,256,256]{2,1,0:T(8,128)S(1)} custom-call(s32[1,16]{1,0:T(1,128)} %target_hbm.1, s32[4]{0:T(128)} %own_hbm.1, s32[8]{0:T(128)} %mom_hbm.1, s32[8]{0:T(128)} %freq_hbm.1, s32[16,16]{1,0:T(8,128)} %sum_hbm.1, f32[1024,1024]{1,0:T(8,128)} %bitcast.6, bf16[4,1024,256]{2,1,0:T(8,128)(2,1)} %bitcast.7, s32[4,256]{1,0:T(4,128)} %bitcast.9, ...), custom_call_target="tpu_custom_call" | custom-call | tf_op jit(solution)/shard_map/exchange/pallas_call | solution.py:286
  28.6 1.0 %copy.13 = f32[1,4,256,256]{3,2,1,0:T(8,128)} copy(f32[1,4,256,256]{3,2,1,0:T(8,128)S(1)} %bitcast.5) | data formatting | bytes 2097152

commit v4 on v3

--- a/solution.py
+++ b/solution.py
@@ -41,14 +41,22 @@
     slots = out_ref.shape[0]
     chunks = [(h, c) for h in range(halves) for c in range(cols)]
     pairs = list(range(1, groups))
-
-    def partner(i):
-        place, bit = grp, 1
+    hold = g_v.shape[2]
+    edge = (groups - hold) // 2
+    me = lax.rem(grp - edge + groups, hold)
+    holder = (grp >= edge) & (grp < edge + hold)
+    outside = jnp.logical_not(holder)
+
+    def flip(start, i):
+        place, bit = start, 1
         while bit <= i:
             if i & bit:
-                place = place + bit - 2 * bit * lax.rem(grp // bit, 2)
+                place = place + bit - 2 * bit * lax.rem(start // bit, 2)
             bit *= 2
         return place
+
+    def partner(i):
+        return flip(grp, i)
 
     def group_peer(i):
         return {"grp": partner(i), "blk": blk}
@@ -131,18 +139,19 @@
         t = nn(jnp.concatenate([wh, wl], axis=0), zh_v[...])
         g = t[:kh] + t[kh:] + nn(wh, zl_v[...])
         for c in range(cols):
-            g_v[h, c] = g[:, c * width:(c + 1) * width].reshape(groups, rows, width)
+            g_v[h, c] = g[:, c * width:(c + 1) * width].reshape(hold, rows, width)
 
     def first(k, i):
         h, c = chunks[k]
-        return pltpu.make_async_remote_copy(
-            g_v.at[h, c, partner(i)], spread[k].at[grp], s1.at[0], r1.at[k],
-            device_id=group_peer(i), device_id_type=MESH)
+        q = flip(me, i)
+        return pltpu.make_async_remote_copy(
+            g_v.at[h, c, q], spread[k].at[grp], s1.at[0], r1.at[k],
+            device_id={"grp": q + edge, "blk": blk}, device_id_type=MESH)
 
     def second(k, i):
         h, c = chunks[k]
         return pltpu.make_async_remote_copy(
-            arranged.at[h, c, partner(i)], seen.at[blk, h, c, grp], s2.at[0], r2.at[k],
+            arranged.at[h, c, partner(i)], seen.at[blk, h, c, me], s2.at[0], r2.at[k],
             device_id=group_peer(i), device_id_type=MESH)
 
     def third(k, j):
@@ -154,16 +163,24 @@
     def across(k, i, j):
         h, c = chunks[k]
         return pltpu.make_async_remote_copy(
-            arranged.at[h, c, partner(i)], seen.at[blk, h, c, grp], s3.at[0], r3.at[j, k],
+            arranged.at[h, c, partner(i)], seen.at[blk, h, c, me], s3.at[0], r3.at[j, k],
             device_id={"grp": partner(i), "blk": lax.rem(blk + j, blocks)}, device_id_type=MESH)
 
-    def pieces(k, recv, send):
-        h, c = chunks[k]
-        return pltpu.make_async_remote_copy(
-            arranged.at[h, c, pl.ds(0, groups - 1)], spread[k].at[pl.ds(0, groups - 1)], send, recv,
+    def bytes_of(count, recv, send):
+        return pltpu.make_async_remote_copy(
+            arranged.at[0, 0, pl.ds(0, count)], arranged.at[0, 0, pl.ds(0, count)], send, recv,
             device_id=block_peer(1), device_id_type=MESH)
 
-    direct = (2, 3)
+    direct = [len(chunks) - 1]
+
+    def arrived(k):
+        @pl.when(holder)
+        def _():
+            bytes_of(hold - 1, r2.at[k], s2.at[0]).wait_recv()
+
+        @pl.when(outside)
+        def _():
+            bytes_of(hold, r2.at[k], s2.at[0]).wait_recv()
 
     copy_l.wait()
     copy_u[number - 1].wait()
@@ -190,9 +207,16 @@
             for i in reversed(range(number)):
                 w = apply(h, w, i)
             finish(h, *split(w))
-        for i in pairs:
+        for i in range(1, hold):
             first(k, i).start()
-        spread[k][grp] = g_v[h, c, grp]
+
+        @pl.when(outside)
+        def _():
+            first(k, 0).start()
+
+        @pl.when(holder)
+        def _():
+            spread[k][grp] = g_v[h, c, me]
 
     for c in small:
         c.wait()
@@ -216,28 +240,30 @@
             hit = jnp.where(base == sum_ref[kappa, q] * nw, 1.0, 0.0).astype(BF16)
             perm_v[j * kw + kappa * nw:j * kw + (kappa + 1) * nw, :] = hit
 
-    for k, (h, c) in enumerate(chunks):
-        pieces(k, r1.at[k], s1.at[0]).wait_recv()
-        for i in pairs:
-            a = partner(i)
-            arranged[h, c, a] = spread[k][source[a]]
-            second(k, i).start()
+    @pl.when(holder)
+    def _():
+        for k, (h, c) in enumerate(chunks):
+            bytes_of(groups - 1, r1.at[k], s1.at[0]).wait_recv()
+            for i in pairs:
+                a = partner(i)
+                arranged[h, c, a] = spread[k][source[a]]
+                second(k, i).start()
+                if k in direct:
+                    for j in range(1, blocks):
+                        across(k, i, j).start()
+            mine = spread[k][source[grp]]
+            seen[blk, h, c, me] = mine
             if k in direct:
+                arranged[h, c, grp] = mine
                 for j in range(1, blocks):
-                    across(k, i, j).start()
-        mine = spread[k][source[grp]]
-        seen[blk, h, c, grp] = mine
-        if k in direct:
-            arranged[h, c, grp] = mine
-            for j in range(1, blocks):
-                across(k, 0, j).start()
+                    across(k, 0, j).start()
 
     def other(j):
         return lax.rem(blk + blocks - j, blocks)
 
     for k in range(len(chunks)):
         if k not in direct:
-            pieces(k, r2.at[k], s2.at[0]).wait_recv()
+            arrived(k)
             for j in range(1, blocks):
                 third(k, j).start()
 
@@ -246,7 +272,7 @@
         now = [k for k in range(len(chunks)) if chunks[k][0] == h]
         for k in now:
             if k in direct:
-                pieces(k, r2.at[k], s2.at[0]).wait_recv()
+                arrived(k)
         accumulate(blk, h)
         for j in range(1, blocks):
             for k in now:
@@ -254,10 +280,23 @@
             accumulate(other(j), h)
 
     for k in range(len(chunks)):
-        pieces(k, r1.at[k], s1.at[0]).wait_send()
-        pieces(k, r2.at[k], s2.at[0]).wait_send()
-        for j in range(1, blocks):
-            third(k, j).wait_send()
+        bytes_of(hold - 1, r1.at[k], s1.at[0]).wait_send()
+        if k not in direct:
+            for j in range(1, blocks):
+                third(k, j).wait_send()
+
+    @pl.when(outside)
+    def _():
+        for k in range(len(chunks)):
+            bytes_of(1, r1.at[k], s1.at[0]).wait_send()
+
+    @pl.when(holder)
+    def _():
+        for k in range(len(chunks)):
+            bytes_of(groups - 1, r2.at[k], s2.at[0]).wait_send()
+            if k in direct:
+                for j in range(1, blocks):
+                    bytes_of(groups, r2.at[k], s3.at[0]).wait_send()
 
 
 def shards(
@@ -278,9 +317,10 @@
     order, kw = left_table.shape
     number, rank = updates.shape[2], updates.shape[4]
     hbm = pl.BlockSpec(memory_space=pltpu.HBM)
-    halves = 2 if kw // groups % 16 == 0 else 1
+    hold = groups // 2 if groups % 4 == 0 else groups
+    halves = 2 if kw // hold % 16 == 0 else 1
     cols = 2 if kw % 256 == 0 else 1
-    rows, width = kw // groups // halves, kw // cols
+    rows, width = kw // hold // halves, kw // cols
     slots = g4_prior.shape[1]
     room = 4 * slots * kw * kw
     summed = pl.pallas_call(
@@ -304,9 +344,9 @@
             pltpu.VMEM((order, kw), BF16),
             pltpu.VMEM((order, kw), BF16),
             pltpu.VMEM((order, kw), BF16),
+            pltpu.VMEM((halves, cols, hold, rows, width), F32),
             pltpu.VMEM((halves, cols, groups, rows, width), F32),
-            pltpu.VMEM((halves, cols, groups, rows, width), F32),
-            pltpu.VMEM((blocks, halves, cols, groups, rows, width), F32),
+            pltpu.VMEM((blocks, halves, cols, hold, rows, width), F32),
             pltpu.VMEM((slots * kw, kw), BF16),
             pltpu.VMEM((blocks, slots, kw, kw), F32),
             pltpu.SMEM((groups,), jnp.int32),

time: 29.7 us -> 29.2 us (0.983)
  Pallas kernels: 28.6 us -> 28.1 us
    pallas_call x1, Pallas kernels: 28.6 us -> 28.1 us  [shards(): pl.pallas_call(functools.partial(exchange_kernel, groups, blocks), out_sh...]
where the time goes in v4:
time: 29.2 us; the launch traced here: 29.1 us
  Pallas kernels  28.1 us (96%)
  local copies, waits for them, and re-layouts  0.97 us (3%)
    pallas_call x1, Pallas kernels, shards(): pl.pallas_call(functools.partial(exchange_kernel, groups, blocks), out_sh...  28.1 us
    unnamed x1, local copies, waits for them, and re-layouts  0.97 us

profile of v4, /device:TPU:0, one launch (start us, length us, event | category | flops | bytes accessed | tf_op | source)
XLA Modules:
  0.0 29.1 jit_solution(2186250001496372390)
XLA Ops:
  0.0 28.1 %exchange.1 = f32[4,256,256]{2,1,0:T(8,128)S(1)} custom-call(s32[1,16]{1,0:T(1,128)} %target_hbm.1, s32[4]{0:T(128)} %own_hbm.1, s32[8]{0:T(128)} %mom_hbm.1, s32[8]{0:T(128)} %freq_hbm.1, s32[16,16]{1,0:T(8,128)} %sum_hbm.1, f32[1024,1024]{1,0:T(8,128)} %bitcast.6, bf16[4,1024,256]{2,1,0:T(8,128)(2,1)} %bitcast.7, s32[4,256]{1,0:T(4,128)} %bitcast.9, ...), custom_call_target="tpu_custom_call" | custom-call | tf_op jit(solution)/shard_map/exchange/pallas_call | solution.py:326
  28.1 1.0 %copy.13 = f32[1,4,256,256]{3,2,1,0:T(8,128)} copy(f32[1,4,256,256]{3,2,1,0:T(8,128)S(1)} %bitcast.5) | data formatting | bytes 2097152

commit v5 on v4

--- a/solution.py
+++ b/solution.py
@@ -247,10 +247,10 @@
             for i in pairs:
                 a = partner(i)
                 arranged[h, c, a] = spread[k][source[a]]
-                second(k, i).start()
                 if k in direct:
                     for j in range(1, blocks):
                         across(k, i, j).start()
+                second(k, i).start()
             mine = spread[k][source[grp]]
             seen[blk, h, c, me] = mine
             if k in direct:

time: 29.2 us -> 29.1 us (level)
  no operation moved by 1% of the time
where the time goes in v5:
time: 29.1 us; the launch traced here: 29 us
  Pallas kernels  28 us (96%)
  local copies, waits for them, and re-layouts  0.97 us (3%)
    pallas_call x1, Pallas kernels, shards(): pl.pallas_call(functools.partial(exchange_kernel, groups, blocks), out_sh...  28 us
    unnamed x1, local copies, waits for them, and re-layouts  0.97 us

profile of v5, /device:TPU:0, one launch (start us, length us, event | category | flops | bytes accessed | tf_op | source)
XLA Modules:
  0.0 29.0 jit_solution(16493428015427050656)
XLA Ops:
  0.0 28.0 %exchange.1 = f32[4,256,256]{2,1,0:T(8,128)S(1)} custom-call(s32[1,16]{1,0:T(1,128)} %target_hbm.1, s32[4]{0:T(128)} %own_hbm.1, s32[8]{0:T(128)} %mom_hbm.1, s32[8]{0:T(128)} %freq_hbm.1, s32[16,16]{1,0:T(8,128)} %sum_hbm.1, f32[1024,1024]{1,0:T(8,128)} %bitcast.6, bf16[4,1024,256]{2,1,0:T(8,128)(2,1)} %bitcast.7, s32[4,256]{1,0:T(4,128)} %bitcast.9, ...), custom_call_target="tpu_custom_call" | custom-call | tf_op jit(solution)/shard_map/exchange/pallas_call | solution.py:326
  28.0 1.0 %copy.13 = f32[1,4,256,256]{3,2,1,0:T(8,128)} copy(f32[1,4,256,256]{3,2,1,0:T(8,128)S(1)} %bitcast.5) | data formatting | bytes 2097152
